TPU v7x, 512 devices: a whole 4x8x8 slice. The times are simulated.
512 devices in a mesh: gz: 16 (over y, x_hi), gy: 32 (over z, x_lo, core).
Axes of the slice: x: 4 (x_hi: 2, x_lo: 2; x = x_hi * 2 + x_lo), y: 8, z: 8, core: 2. Of those that a mesh axis runs over, the one named last changes fastest.
Arguments:
- field_b: float32 [3, 2, 2048, 2048], P(None, None, 'gy', 'gz'), may hold values from -6 to 6
- density: float32 [2, 2048, 2048], P(None, 'gy', 'gz'), may hold values from 0.5 to 2
- level_y: int32 [2048], P('gy'), may hold values from 0 to 7
- level_z: int32 [2048], P('gz'), may hold values from 0 to 7
- bins: int32 [1024, 2048], P(('gz', 'gy')), may hold values from 0 to 1023
Outputs:
- emf: bfloat16 [3, 2, 2048, 2048], P(None, None, 'gy', 'gz')
- mode_power: float32 [1024, 2048], P(('gz', 'gy'))
- spectrum: float32 [1024], replicated
All inputs are finite; a program needn't handle non-finite values.
Results may differ from a plain program's by a relative error of at most 0.0035.
Values may be sent and summed in bfloat16 or wider, within the bound.
No kernel may reach another device: no remote copies, remote signals or barrier semaphores. Data moves between devices by JAX's collectives and lax.ppermute only.
A program may use at most 64 MiB of HBM per device.

v0:
```python
import math
import jax
import jax.numpy as jnp
from jax import lax
from jax.sharding import PartitionSpec as P

NY = 2048
NZ = 2048
NB = 1024
KZ = 1024


def extended(cells, sides, width):
    for axis, dim in sides:
        count = lax.axis_size(axis)
        head = lax.slice_in_dim(cells, 0, width, axis=dim)
        tail = lax.slice_in_dim(cells, cells.shape[dim] - width, cells.shape[dim], axis=dim)
        cells = jnp.concatenate(
            [
                lax.ppermute(tail, axis, [(i, (i + 1) % count) for i in range(count)]),
                cells,
                lax.ppermute(head, axis, [((i + 1) % count, i) for i in range(count)]),
            ],
            axis=dim,
        )
    return cells


def metric(level):
    return 1.0 / (1.0 + 0.25 * level.astype(jnp.float32))


def twiddle(positions, modes, length):
    phase = positions[:, None] * modes[None, :] % length
    angle = phase.astype(jnp.float32) * (2.0 * math.pi / length)
    factor = 1.0 / math.sqrt(length)
    return (
        (jnp.cos(angle) * factor).astype(jnp.bfloat16),
        (jnp.sin(angle) * factor).astype(jnp.bfloat16),
    )


def on_device(field_b, density, level_y, level_z, bins):
    planes = field_b.shape[1]
    y_local = field_b.shape[2]
    metric_y = metric(level_y)[None, None, :, None]
    metric_z = metric(level_z)[None, None, None, :]
    padded = extended(field_b, (("gz", 3), ("gy", 2)), 1)
    grad_y = 0.5 * (padded[:, :, 2:, 1:-1] - padded[:, :, :-2, 1:-1]) * metric_y
    grad_z = 0.5 * (padded[:, :, 1:-1, 2:] - padded[:, :, 1:-1, :-2]) * metric_z
    x_padded = jnp.pad(field_b, ((0, 0), (1, 1), (0, 0), (0, 0)))
    grad_x = 0.5 * (x_padded[:, 2:] - x_padded[:, :-2])
    cur_x = grad_y[2] - grad_z[1]
    cur_y = grad_z[0] - grad_x[2]
    cur_z = grad_x[1] - grad_y[0]
    e_x = (cur_y * field_b[2] - cur_z * field_b[1]) / density
    e_y = (cur_z * field_b[0] - cur_x * field_b[2]) / density
    e_z = (cur_x * field_b[1] - cur_y * field_b[0]) / density
    emf = jnp.stack([e_x, e_y, e_z]).astype(jnp.bfloat16)
    kz_dev = KZ // lax.axis_size("gz")
    z_pos = jnp.arange(NZ, dtype=jnp.int32)
    k_start = lax.axis_index("gz") * kz_dev
    z_cos, z_sin = twiddle(z_pos, k_start + jnp.arange(kz_dev, dtype=jnp.int32), NZ)
    table_z = jnp.concatenate([z_cos, -z_sin], axis=1)
    summed = jnp.einsum(
        "cxyz,zk->kcxy",
        lax.all_gather(emf, "gz", axis=3, tiled=True),
        table_z,
        preferred_element_type=jnp.float32,
    )
    z_modes = summed.reshape(2, kz_dev, 3, planes, y_local).astype(jnp.bfloat16)
    spread = lax.all_to_all(z_modes, "gy", split_axis=1, concat_axis=4, tiled=True)
    k_few = spread.shape[1]
    count = k_few * 3 * planes
    lhs_rows = spread.reshape(2 * count, NY)
    y_block = min(512, NY)
    y_pos = jnp.arange(NY, dtype=jnp.int32)

    def power_block(block_id):
        y_cos, y_sin = twiddle(y_pos, block_id * y_block + jnp.arange(y_block, dtype=jnp.int32), NY)
        product = jnp.dot(
            lhs_rows, jnp.concatenate([y_cos, y_sin], axis=1), preferred_element_type=jnp.float32
        )
        re_cos = product[:count, :y_block]
        re_sin = product[:count, y_block:]
        im_cos = product[count:, :y_block]
        im_sin = product[count:, y_block:]
        real_part = re_cos + im_sin
        imag_part = im_cos - re_sin
        power = (real_part * real_part + imag_part * imag_part).reshape(k_few, 3 * planes, y_block)
        return jnp.sum(power, axis=1) / (3 * planes)

    blocks = lax.map(power_block, jnp.arange(NY // y_block, dtype=jnp.int32))
    mode_power = blocks.transpose(1, 0, 2).reshape(k_few, NY)
    local_bins = jax.ops.segment_sum(mode_power.reshape(-1), bins.reshape(-1), num_segments=NB) * (
        NB / (KZ * NY)
    )
    spectrum = lax.psum(local_bins, ("gz", "gy"))
    return (emf, mode_power, spectrum)


def solution(mesh):
    placed = (
        P(None, None, "gy", "gz"),
        P(None, "gy", "gz"),
        P("gy"),
        P("gz"),
        P(("gz", "gy"), None),
    )
    return jax.shard_map(
        on_device,
        mesh=mesh,
        in_specs=placed,
        out_specs=(P(None, None, "gy", "gz"), P(("gz", "gy"), None), P()),
        check_vma=False,
    )
```

profile of v0, /device:TPU:1, one launch (start us, length us, event | category | flops | bytes accessed | tf_op | source)
XLA Modules:
  0.0 355.4 jit_solution(7134544797630249698)
XLA Ops:
  7.2 0.0 copy-start
  7.2 0.0 all-gather.2.cloned.1.call-start
  7.2 1.2 fusion.43
  8.4 8.4 %collective-permute-start = (f32[3,2,64,1]{3,2,1,0:T(8,128)S(1)}, f32[3,2,64,1]{3,2,1,0:T(8,128)S(1)}, u32[]{:S(2)}, u32[]{:S(2)}) collective-permute-start(f32[3,2,64,1]{3,2,1,0:T(8,128)S(1)} %get-tuple-element.98), channel_id=1, source_target_pairs={{32,0},{64,32},{96,64},{128,96},{160,128},{192,160},{224,192},{256... | collective-permute-start | bytes 4616 | tf_op jit(solution)/shard_map/ppermute | solution.py:22
  16.8 1.9 collective-permute-start.1
  18.7 0.7 divide_multiply_fusion
  19.4 1.0 collective-permute-done
  20.4 7.4 %collective-permute-done.1 = f32[3,2,64,1]{3,2,1,0:T(8,128)S(1)} collective-permute-done((f32[3,2,64,1]{3,2,1,0:T(8,128)S(1)}, f32[3,2,64,1]{3,2,1,0:T(8,128)S(1)}, u32[]{:S(2)}, u32[]{:S(2)}) %collective-permute-start.1) | collective-permute-done | bytes 1568 | tf_op jit(solution)/shard_map/ppermute | solution.py:20
  27.8 0.9 pad_maximum_fusion.11
  28.6 3.8 %collective-permute-start.2 = (f32[3,2,1,130]{3,2,1,0:T(1,128)S(1)}, f32[3,2,1,130]{3,2,1,0:T(1,128)S(1)}, u32[]{:S(2)}, u32[]{:S(2)}) collective-permute-start(f32[3,2,1,130]{3,2,1,0:T(1,128)S(1)} %get-tuple-element.95), channel_id=1, source_target_pairs={{1,0},{2,1},{3,2},{4,3},{5,4},{6,5},{7,6},{8,7},{9,8},{10,9},{11,1... | collective-permute-start | bytes 9368 | tf_op jit(solution)/shard_map/ppermute | solution.py:22
  32.4 2.1 collective-permute-start.3
  34.6 0.7 divide_multiply_fusion.1
  35.2 0.0 collective-permute-done.2
  35.2 7.1 %collective-permute-done.3 = f32[3,2,1,130]{3,2,1,0:T(1,128)S(1)} collective-permute-done((f32[3,2,1,130]{3,2,1,0:T(1,128)S(1)}, f32[3,2,1,130]{3,2,1,0:T(1,128)S(1)}, u32[]{:S(2)}, u32[]{:S(2)}) %collective-permute-start.3) | collective-permute-done | bytes 3152 | tf_op jit(solution)/shard_map/ppermute | solution.py:20
  42.3 1.7 fusion.31
  44.0 0.0 copy-done
  44.0 0.0 copy-done.1
  44.0 0.1 fusion.37
  44.1 0.7 pad_maximum_fusion.8
  44.8 0.0 all-gather.2.cloned.1.call-update
  44.8 2.1 fusion.27
  46.9 2.1 multiply_convert_fusion.3
  49.1 75.1 %all-gather.2.cloned.1.call-done = bf16[3,2,64,2048]{3,2,1,0:T(8,128)(2,1)} async-done(((bf16[3,2,64,128]{3,2,1,0:T(8,128)(2,1)}), bf16[3,2,64,2048]{3,2,1,0:T(8,128)(2,1)}) %all-gather.2.cloned.1.call-update) | async-done | bytes 1572880 | tf_op jit(solution)/shard_map/all_gather | solution.py:67
  124.2 2.0 convolution_convert_fusion
  126.1 0.1 convert_element_type.48
  126.3 0.2 copy.23
  126.4 0.8 reshape.73
  127.2 11.8 %all-to-all-start = ((bf16[32,2,768]{2,1,0:T(2,128)(2,1)}), bf16[32,2,768]{2,1,0:T(2,128)(2,1)S(1)}, u32[]{:S(2)}, u32[]{:S(2)}) async-start(bf16[32,2,768]{2,1,0:T(2,128)(2,1)} %reshape.73), calls=%async_computation | async-start | bytes 196608 | tf_op jit(solution)/shard_map/all_to_all | solution.py:72
  139.0 0.0 copy-done.2
  139.0 8.7 %all-to-all-done = bf16[32,2,768]{2,1,0:T(2,128)(2,1)S(1)} async-done(((bf16[32,2,768]{2,1,0:T(2,128)(2,1)}), bf16[32,2,768]{2,1,0:T(2,128)(2,1)S(1)}, u32[]{:S(2)}, u32[]{:S(2)}) %all-to-all-start) | async-done | bytes 98336 | tf_op jit(solution)/shard_map/all_to_all | solution.py:72
  147.8 0.2 reshape.74
  148.0 0.2 reshape.58
  148.3 76.5 %while.13 = (s32[]{:T(128)}, f32[4,2,512]{2,1,0:T(2,128)S(1)}, s32[4]{0:T(128)S(1)}, bf16[24,2048]{1,0:T(8,128)(2,1)S(1)}, s32[]{:T(128)}, /*index=5*/s32[1]{0:T(128)}, f32[]{:T(128)}) while((s32[]{:T(128)}, f32[4,2,512]{2,1,0:T(2,128)S(1)}, s32[4]{0:T(128)S(1)}, bf16[24,2048]{1,0:T(8,128)(2,1)S(1)}, s32[]{:T(128)}, ...), condition=%wide.region_2.3_spmd.clone, body=%wide.region_0.2_spmd.clone.sunk | while | flops 127963648 | bytes 8798321 | solution.py:93
  148.3 0.6 dynamic_slice.9
  149.5 17.1 %multiply_convert_fusion.5 = (bf16[2048,512]{1,0:T(8,128)(2,1)S(1)}, bf16[2048,512]{1,0:T(8,128)(2,1)S(1)}) fusion(s32[512]{0:T(512)S(1)} %iota_add_fusion.3), kind=kLoop, calls=%fused_computation.16.clone.1 | loop fusion | flops 18874368 | bytes 4196352 | tf_op jit(solution)/shard_map/while/body/eval_jaxpr/convert_element_type | solution.py:38
  166.6 0.6 fusion.52
  167.4 0.6 dynamic_slice.9
  168.6 17.1 %multiply_convert_fusion.5 = (bf16[2048,512]{1,0:T(8,128)(2,1)S(1)}, bf16[2048,512]{1,0:T(8,128)(2,1)S(1)}) fusion(s32[512]{0:T(512)S(1)} %iota_add_fusion.3), kind=kLoop, calls=%fused_computation.16.clone.1 | loop fusion | flops 18874368 | bytes 4196352 | tf_op jit(solution)/shard_map/while/body/eval_jaxpr/convert_element_type | solution.py:38
  185.8 0.6 fusion.52
  186.5 0.6 dynamic_slice.9
  187.8 17.1 %multiply_convert_fusion.5 = (bf16[2048,512]{1,0:T(8,128)(2,1)S(1)}, bf16[2048,512]{1,0:T(8,128)(2,1)S(1)}) fusion(s32[512]{0:T(512)S(1)} %iota_add_fusion.3), kind=kLoop, calls=%fused_computation.16.clone.1 | loop fusion | flops 18874368 | bytes 4196352 | tf_op jit(solution)/shard_map/while/body/eval_jaxpr/convert_element_type | solution.py:38
  204.9 0.6 fusion.52
  205.6 0.6 dynamic_slice.9
  206.9 17.1 %multiply_convert_fusion.5 = (bf16[2048,512]{1,0:T(8,128)(2,1)S(1)}, bf16[2048,512]{1,0:T(8,128)(2,1)S(1)}) fusion(s32[512]{0:T(512)S(1)} %iota_add_fusion.3), kind=kLoop, calls=%fused_computation.16.clone.1 | loop fusion | flops 18874368 | bytes 4196352 | tf_op jit(solution)/shard_map/while/body/eval_jaxpr/convert_element_type | solution.py:38
  224.0 0.6 fusion.52
  224.8 0.0 copy-start.3
  224.8 28.8 %scatter_custom_fusion = f32[1024]{0:T(1024)S(1)} fusion(s32[4096]{0:T(1024)S(1)} %bitcast.67, f32[4096]{0:T(1024)S(1)} %bitcast.70, f32[]{:T(128)} %constant.93.clone.1), kind=kCustom, calls=%fused_computation.77 | custom fusion | flops 4096 | bytes 4100 | tf_op jit(solution)/shard_map/scatter-add | solution.py:95
  253.6 95.0 %psum.7 = f32[1024]{0:T(1024)} all-reduce(f32[1024]{0:T(1024)S(1)} %broadcast_multiply_fusion), channel_id=1, replica_groups=mesh['gz'=16,'gy'=32] {'gz','gy'}, use_global_device_ids=true, to_apply=%region_4.5 | all-reduce | flops 1024 | bytes 8192 | tf_op jit(solution)/shard_map/psum | solution.py:98
  (32 shorter events, 0.4 us)
Async XLA Ops:
  7.2 36.9 %copy-start = (f32[3,2,64,128]{3,2,1,0:T(8,128)S(1)}, f32[3,2,64,128]{3,2,1,0:T(8,128)}, u32[]{:S(2)}) copy-start(f32[3,2,64,128]{3,2,1,0:T(8,128)} %param.7) | copy-start | bytes 589828
  7.2 36.9 %copy-start.1 = (f32[2,64,128]{2,1,0:T(8,128)S(1)}, f32[2,64,128]{2,1,0:T(8,128)}, u32[]{:S(2)}) copy-start(f32[2,64,128]{2,1,0:T(8,128)} %param.8) | copy-start | bytes 196612
  7.2 117.0 %all-gather.2.cloned.1.call-start = ((), (), s32[]{:S(2)}) async-start(), calls=%async_computation.1 | async-start | bytes 1671168 | tf_op jit(solution)/shard_map/all_gather | solution.py:67
  8.4 11.9 %collective-permute-start = (f32[3,2,64,1]{3,2,1,0:T(8,128)S(1)}, f32[3,2,64,1]{3,2,1,0:T(8,128)S(1)}, u32[]{:S(2)}, u32[]{:S(2)}) collective-permute-start(f32[3,2,64,1]{3,2,1,0:T(8,128)S(1)} %get-tuple-element.98), channel_id=1, source_target_pairs={{32,0},{64,32},{96,64},{128,96},{160,128},{192,160},{224,192},{256... | collective-permute-start | bytes 4616 | tf_op jit(solution)/shard_map/ppermute | solution.py:22
  16.8 11.0 %collective-permute-start.1 = (f32[3,2,64,1]{3,2,1,0:T(8,128)S(1)}, f32[3,2,64,1]{3,2,1,0:T(8,128)S(1)}, u32[]{:S(2)}, u32[]{:S(2)}) collective-permute-start(f32[3,2,64,1]{3,2,1,0:T(8,128)S(1)} %get-tuple-element.99), channel_id=1, source_target_pairs={{0,32},{32,64},{64,96},{96,128},{128,160},{160,192},{192,224},{224... | collective-permute-start | bytes 4616 | tf_op jit(solution)/shard_map/ppermute | solution.py:20
  28.6 6.6 %collective-permute-start.2 = (f32[3,2,1,130]{3,2,1,0:T(1,128)S(1)}, f32[3,2,1,130]{3,2,1,0:T(1,128)S(1)}, u32[]{:S(2)}, u32[]{:S(2)}) collective-permute-start(f32[3,2,1,130]{3,2,1,0:T(1,128)S(1)} %get-tuple-element.95), channel_id=1, source_target_pairs={{1,0},{2,1},{3,2},{4,3},{5,4},{6,5},{7,6},{8,7},{9,8},{10,9},{11,1... | collective-permute-start | bytes 9368 | tf_op jit(solution)/shard_map/ppermute | solution.py:22
  32.4 9.9 %collective-permute-start.3 = (f32[3,2,1,130]{3,2,1,0:T(1,128)S(1)}, f32[3,2,1,130]{3,2,1,0:T(1,128)S(1)}, u32[]{:S(2)}, u32[]{:S(2)}) collective-permute-start(f32[3,2,1,130]{3,2,1,0:T(1,128)S(1)} %get-tuple-element.96), channel_id=1, source_target_pairs={{0,1},{1,2},{2,3},{3,4},{4,5},{5,6},{6,7},{7,8},{8,9},{9,10},{10,1... | collective-permute-start | bytes 9368 | tf_op jit(solution)/shard_map/ppermute | solution.py:20
  44.8 94.3 %copy-start.2 = (s32[2,2048]{1,0:T(2,128)S(1)}, s32[2,2048]{1,0:T(2,128)}, u32[]{:S(2)}) copy-start(s32[2,2048]{1,0:T(2,128)} %param.11) | copy-start | bytes 49156
  127.2 20.5 %all-to-all-start = ((bf16[32,2,768]{2,1,0:T(2,128)(2,1)}), bf16[32,2,768]{2,1,0:T(2,128)(2,1)S(1)}, u32[]{:S(2)}, u32[]{:S(2)}) async-start(bf16[32,2,768]{2,1,0:T(2,128)(2,1)} %reshape.73), calls=%async_computation | async-start | bytes 196608 | tf_op jit(solution)/shard_map/all_to_all | solution.py:72
  224.8 123.8 %copy-start.3 = (f32[4,2,512]{2,1,0:T(2,128)}, f32[4,2,512]{2,1,0:T(2,128)S(1)}, u32[]{:S(2)}) copy-start(f32[4,2,512]{2,1,0:T(2,128)S(1)} %get-tuple-element.69) | copy-start | bytes 49156
Sparse Core Ops, SparseCore 0:
  44.9 79.1 all-gather.1
where the time goes:
time: 356 us; the launch traced here: 355 us
  other arithmetic  106 us (30%)
  waiting for transfers between devices  99.3 us (28%)
  blocking collectives  95 us (27%)
  starting transfers between devices  28 us (8%)
  between operations  14.3 us (4%)
  local copies, waits for them, and re-layouts  5.11 us (1%)
  matrix products  4.56 us (1%)
    psum x1, blocking collectives, on_device(): spectrum = lax.psum(local_bins, ('gz', 'gy'))  95 us
    all_gather x1, waiting for transfers between devices, on_device(): lax.all_gather(emf, 'gz', axis=3, tiled=True)  75.1 us
    convert_element_type x5, other arithmetic, twiddle(): (jnp.cos(angle) * factor).astype(jnp.bfloat16)  70.6 us
    scatter-add x1, other arithmetic, on_device(): jax.ops.segment_sum(mode_power.reshape(-1), bins.reshape(-1), num_segment...  28.8 us
    ppermute x2, waiting for transfers between devices, extended(): lax.ppermute(tail, axis, [(i, (i + 1) % count) for i in range(count)])  14.5 us
    ppermute x2, starting transfers between devices, extended(): lax.ppermute(head, axis, [((i + 1) % count, i) for i in range(count)])  12.2 us
    all_to_all x1, starting transfers between devices, on_device(): lax.all_to_all(z_modes, 'gy', split_axis=1, concat_axis=4, tiled=True)  11.8 us
    all_to_all x1, waiting for transfers between devices, on_device(): lax.all_to_all(z_modes, 'gy', split_axis=1, concat_axis=4, tiled=True)  8.73 us
  transfers between devices with their start and end apart: 6, of which 5 were waited for; matrix products, arithmetic and copies ran while one was open for 2% of the time, Pallas kernels for 0%

commit v1 on v0

--- a/solution.py
+++ b/solution.py
@@ -64,7 +64,7 @@
     table_z = jnp.concatenate([z_cos, -z_sin], axis=1)
     summed = jnp.einsum(
         "cxyz,zk->kcxy",
-        lax.all_gather(emf, "gz", axis=3, tiled=True),
+        jnp.concatenate(lax.all_to_all(jnp.stack([emf] * lax.axis_size("gz")), "gz", 0, 0), axis=3),
         table_z,
         preferred_element_type=jnp.float32,
     )

time: 356 us -> 307 us (0.86)
  waiting for transfers between devices: 99.3 us -> 54.3 us
  between operations: 14.3 us -> 0.92 us
  starting transfers between devices: 28 us -> 34.5 us
    all_gather x1 -> x0, waiting for transfers between devices: 75.1 us -> none  [on_device(): lax.all_gather(emf, 'gz', axis=3, tiled=True)]
    all_to_all x0 -> x1, waiting for transfers between devices: none -> 30.1 us  [on_device(): lax.all_to_all(jnp.stack([emf] * lax.axis_size('gz')), 'gz', 0, 0)]
    all_to_all x0 -> x1, starting transfers between devices: none -> 6.8 us  [on_device(): lax.all_to_all(jnp.stack([emf] * lax.axis_size('gz')), 'gz', 0, 0)]
where the time goes in v1:
time: 307 us; the launch traced here: 306 us
  other arithmetic  107 us (35%)
  blocking collectives  94.1 us (31%)
  waiting for transfers between devices  54.3 us (18%)
  starting transfers between devices  34.5 us (11%)
  local copies, waits for them, and re-layouts  8.31 us (3%)
  matrix products  4.53 us (1%)
    psum x1, blocking collectives, on_device(): spectrum = lax.psum(local_bins, ('gz', 'gy'))  94.1 us
    convert_element_type x5, other arithmetic, twiddle(): (jnp.cos(angle) * factor).astype(jnp.bfloat16)  70.6 us
    all_to_all x1, waiting for transfers between devices, on_device(): lax.all_to_all(jnp.stack([emf] * lax.axis_size('gz')), 'gz', 0, 0)  30.1 us
    scatter-add x1, other arithmetic, on_device(): jax.ops.segment_sum(mode_power.reshape(-1), bins.reshape(-1), num_segment...  28.8 us
    ppermute x2, waiting for transfers between devices, extended(): lax.ppermute(tail, axis, [(i, (i + 1) % count) for i in range(count)])  14.5 us
    ppermute x2, starting transfers between devices, extended(): lax.ppermute(head, axis, [((i + 1) % count, i) for i in range(count)])  12.2 us
    all_to_all x1, starting transfers between devices, on_device(): lax.all_to_all(z_modes, 'gy', split_axis=1, concat_axis=4, tiled=True)  11.5 us
    all_to_all x1, waiting for transfers between devices, on_device(): lax.all_to_all(z_modes, 'gy', split_axis=1, concat_axis=4, tiled=True)  8.73 us
  transfers between devices with their start and end apart: 6, of which 5 were waited for; matrix products, arithmetic and copies ran while one was open for 2% of the time, Pallas kernels for 0%

profile of v1, /device:TPU:1, one launch (start us, length us, event | category | flops | bytes accessed | tf_op | source)
XLA Modules:
  0.0 306.0 jit_solution(15833572891760499516)
XLA Ops:
  0.6 0.0 copy-start
  0.7 1.2 fusion.40
  1.8 8.4 %collective-permute-start = (f32[3,2,64,1]{3,2,1,0:T(8,128)S(1)}, f32[3,2,64,1]{3,2,1,0:T(8,128)S(1)}, u32[]{:S(2)}, u32[]{:S(2)}) collective-permute-start(f32[3,2,64,1]{3,2,1,0:T(8,128)S(1)} %get-tuple-element.98), channel_id=1, source_target_pairs={{32,0},{64,32},{96,64},{128,96},{160,128},{192,160},{224,192},{256... | collective-permute-start | bytes 4616 | tf_op jit(solution)/shard_map/ppermute | solution.py:22
  10.2 1.9 collective-permute-start.1
  12.2 0.7 divide_multiply_fusion
  12.8 1.0 collective-permute-done
  13.8 7.4 %collective-permute-done.1 = f32[3,2,64,1]{3,2,1,0:T(8,128)S(1)} collective-permute-done((f32[3,2,64,1]{3,2,1,0:T(8,128)S(1)}, f32[3,2,64,1]{3,2,1,0:T(8,128)S(1)}, u32[]{:S(2)}, u32[]{:S(2)}) %collective-permute-start.1) | collective-permute-done | bytes 1568 | tf_op jit(solution)/shard_map/ppermute | solution.py:20
  21.2 0.9 pad_maximum_fusion.12
  22.0 3.8 %collective-permute-start.2 = (f32[3,2,1,130]{3,2,1,0:T(1,128)S(1)}, f32[3,2,1,130]{3,2,1,0:T(1,128)S(1)}, u32[]{:S(2)}, u32[]{:S(2)}) collective-permute-start(f32[3,2,1,130]{3,2,1,0:T(1,128)S(1)} %get-tuple-element.95), channel_id=1, source_target_pairs={{1,0},{2,1},{3,2},{4,3},{5,4},{6,5},{7,6},{8,7},{9,8},{10,9},{11,1... | collective-permute-start | bytes 9368 | tf_op jit(solution)/shard_map/ppermute | solution.py:22
  25.8 2.1 collective-permute-start.3
  28.0 0.7 divide_multiply_fusion.1
  28.6 0.0 collective-permute-done.2
  28.6 7.1 %collective-permute-done.3 = f32[3,2,1,130]{3,2,1,0:T(1,128)S(1)} collective-permute-done((f32[3,2,1,130]{3,2,1,0:T(1,128)S(1)}, f32[3,2,1,130]{3,2,1,0:T(1,128)S(1)}, u32[]{:S(2)}, u32[]{:S(2)}) %collective-permute-start.3) | collective-permute-done | bytes 3152 | tf_op jit(solution)/shard_map/ppermute | solution.py:20
  35.7 1.7 fusion.29
  37.4 0.1 fusion.35
  37.5 0.0 copy-start.1
  37.5 1.5 stack.18
  39.1 6.8 %all-to-all-start = ((bf16[16,3,2,64,128]{4,3,2,1,0:T(8,128)(2,1)}), bf16[16,3,2,64,128]{4,3,2,1,0:T(8,128)(2,1)S(1)}, u32[]{:S(2)}, u32[]{:S(2)}) async-start(bf16[16,3,2,64,128]{4,3,2,1,0:T(8,128)(2,1)} %stack.18), calls=%async_computation | async-start | bytes 3145728 | tf_op jit(solution)/shard_map/all_to_all | solution.py:67
  45.9 2.1 fusion.25
  48.0 2.1 multiply_convert_fusion.3
  50.2 0.8 pad_maximum_fusion
  51.0 30.1 %all-to-all-done = bf16[16,3,2,64,128]{4,3,2,1,0:T(8,128)(2,1)S(1)} async-done(((bf16[16,3,2,64,128]{4,3,2,1,0:T(8,128)(2,1)}), bf16[16,3,2,64,128]{4,3,2,1,0:T(8,128)(2,1)S(1)}, u32[]{:S(2)}, u32[]{:S(2)}) %all-to-all-start) | async-done | bytes 1572896 | tf_op jit(solution)/shard_map/all_to_all | solution.py:67
  81.1 1.0 copy.13
  82.2 0.7 reshape.92
  82.9 0.0 copy-start.3
  82.9 1.9 convolution_convert_fusion
  84.9 0.2 copy.24
  85.1 0.8 reshape.96
  85.9 11.5 %all-to-all-start.1 = ((bf16[32,2,768]{2,1,0:T(2,128)(2,1)}), bf16[32,2,768]{2,1,0:T(2,128)(2,1)S(1)}, u32[]{:S(2)}, u32[]{:S(2)}) async-start(bf16[32,2,768]{2,1,0:T(2,128)(2,1)} %reshape.96), calls=%async_computation.1 | async-start | bytes 196608 | tf_op jit(solution)/shard_map/all_to_all | solution.py:72
  97.4 8.7 %all-to-all-done.1 = bf16[32,2,768]{2,1,0:T(2,128)(2,1)S(1)} async-done(((bf16[32,2,768]{2,1,0:T(2,128)(2,1)}), bf16[32,2,768]{2,1,0:T(2,128)(2,1)S(1)}, u32[]{:S(2)}, u32[]{:S(2)}) %all-to-all-start.1) | async-done | bytes 98336 | tf_op jit(solution)/shard_map/all_to_all | solution.py:72
  106.1 0.2 reshape.97
  106.4 0.2 reshape.79
  106.6 76.5 %while.13 = (s32[]{:T(128)}, f32[4,2,512]{2,1,0:T(2,128)S(1)}, s32[4]{0:T(128)S(1)}, bf16[24,2048]{1,0:T(8,128)(2,1)S(1)}, s32[]{:T(128)}, /*index=5*/s32[1]{0:T(128)}, f32[]{:T(128)}) while((s32[]{:T(128)}, f32[4,2,512]{2,1,0:T(2,128)S(1)}, s32[4]{0:T(128)S(1)}, bf16[24,2048]{1,0:T(8,128)(2,1)S(1)}, s32[]{:T(128)}, ...), condition=%wide.region_2.3_spmd.clone, body=%wide.region_0.2_spmd.clone.sunk | while | flops 127963648 | bytes 8798321 | solution.py:93
  106.6 0.6 dynamic_slice.9
  107.9 17.1 %multiply_convert_fusion.5 = (bf16[2048,512]{1,0:T(8,128)(2,1)S(1)}, bf16[2048,512]{1,0:T(8,128)(2,1)S(1)}) fusion(s32[512]{0:T(512)S(1)} %iota_add_fusion.3), kind=kLoop, calls=%fused_computation.16.clone.1 | loop fusion | flops 18874368 | bytes 4196352 | tf_op jit(solution)/shard_map/while/body/eval_jaxpr/convert_element_type | solution.py:38
  125.0 0.6 fusion.50
  125.7 0.6 dynamic_slice.9
  127.0 17.1 %multiply_convert_fusion.5 = (bf16[2048,512]{1,0:T(8,128)(2,1)S(1)}, bf16[2048,512]{1,0:T(8,128)(2,1)S(1)}) fusion(s32[512]{0:T(512)S(1)} %iota_add_fusion.3), kind=kLoop, calls=%fused_computation.16.clone.1 | loop fusion | flops 18874368 | bytes 4196352 | tf_op jit(solution)/shard_map/while/body/eval_jaxpr/convert_element_type | solution.py:38
  144.1 0.6 fusion.50
  144.9 0.6 dynamic_slice.9
  146.1 17.1 %multiply_convert_fusion.5 = (bf16[2048,512]{1,0:T(8,128)(2,1)S(1)}, bf16[2048,512]{1,0:T(8,128)(2,1)S(1)}) fusion(s32[512]{0:T(512)S(1)} %iota_add_fusion.3), kind=kLoop, calls=%fused_computation.16.clone.1 | loop fusion | flops 18874368 | bytes 4196352 | tf_op jit(solution)/shard_map/while/body/eval_jaxpr/convert_element_type | solution.py:38
  163.2 0.6 fusion.50
  164.0 0.6 dynamic_slice.9
  165.2 17.1 %multiply_convert_fusion.5 = (bf16[2048,512]{1,0:T(8,128)(2,1)S(1)}, bf16[2048,512]{1,0:T(8,128)(2,1)S(1)}) fusion(s32[512]{0:T(512)S(1)} %iota_add_fusion.3), kind=kLoop, calls=%fused_computation.16.clone.1 | loop fusion | flops 18874368 | bytes 4196352 | tf_op jit(solution)/shard_map/while/body/eval_jaxpr/convert_element_type | solution.py:38
  182.4 0.6 fusion.50
  183.1 0.0 copy-start.4
  183.2 28.8 %scatter_custom_fusion = f32[1024]{0:T(1024)S(1)} fusion(s32[4096]{0:T(1024)S(1)} %bitcast.74, f32[4096]{0:T(1024)S(1)} %bitcast.77, f32[]{:T(128)} %constant.93.clone.1), kind=kCustom, calls=%fused_computation.75 | custom fusion | flops 4096 | bytes 4100 | tf_op jit(solution)/shard_map/scatter-add | solution.py:95
  212.0 94.1 %psum.7 = f32[1024]{0:T(1024)} all-reduce(f32[1024]{0:T(1024)S(1)} %broadcast_multiply_fusion), channel_id=1, replica_groups=mesh['gz'=16,'gy'=32] {'gz','gy'}, use_global_device_ids=true, to_apply=%region_4.5 | all-reduce | flops 1024 | bytes 8192 | tf_op jit(solution)/shard_map/psum | solution.py:98
  (35 shorter events, 0.4 us)
Async XLA Ops:
  0.6 36.8 %copy-start = (f32[3,2,64,128]{3,2,1,0:T(8,128)S(1)}, f32[3,2,64,128]{3,2,1,0:T(8,128)}, u32[]{:S(2)}) copy-start(f32[3,2,64,128]{3,2,1,0:T(8,128)} %param.7) | copy-start | bytes 589828
  0.6 36.8 %copy-start.2 = (f32[2,64,128]{2,1,0:T(8,128)S(1)}, f32[2,64,128]{2,1,0:T(8,128)}, u32[]{:S(2)}) copy-start(f32[2,64,128]{2,1,0:T(8,128)} %param.8) | copy-start | bytes 196612
  1.8 11.9 %collective-permute-start = (f32[3,2,64,1]{3,2,1,0:T(8,128)S(1)}, f32[3,2,64,1]{3,2,1,0:T(8,128)S(1)}, u32[]{:S(2)}, u32[]{:S(2)}) collective-permute-start(f32[3,2,64,1]{3,2,1,0:T(8,128)S(1)} %get-tuple-element.98), channel_id=1, source_target_pairs={{32,0},{64,32},{96,64},{128,96},{160,128},{192,160},{224,192},{256... | collective-permute-start | bytes 4616 | tf_op jit(solution)/shard_map/ppermute | solution.py:22
  10.2 11.0 %collective-permute-start.1 = (f32[3,2,64,1]{3,2,1,0:T(8,128)S(1)}, f32[3,2,64,1]{3,2,1,0:T(8,128)S(1)}, u32[]{:S(2)}, u32[]{:S(2)}) collective-permute-start(f32[3,2,64,1]{3,2,1,0:T(8,128)S(1)} %get-tuple-element.99), channel_id=1, source_target_pairs={{0,32},{32,64},{64,96},{96,128},{128,160},{160,192},{192,224},{224... | collective-permute-start | bytes 4616 | tf_op jit(solution)/shard_map/ppermute | solution.py:20
  22.0 6.6 %collective-permute-start.2 = (f32[3,2,1,130]{3,2,1,0:T(1,128)S(1)}, f32[3,2,1,130]{3,2,1,0:T(1,128)S(1)}, u32[]{:S(2)}, u32[]{:S(2)}) collective-permute-start(f32[3,2,1,130]{3,2,1,0:T(1,128)S(1)} %get-tuple-element.95), channel_id=1, source_target_pairs={{1,0},{2,1},{3,2},{4,3},{5,4},{6,5},{7,6},{8,7},{9,8},{10,9},{11,1... | collective-permute-start | bytes 9368 | tf_op jit(solution)/shard_map/ppermute | solution.py:22
  25.8 9.9 %collective-permute-start.3 = (f32[3,2,1,130]{3,2,1,0:T(1,128)S(1)}, f32[3,2,1,130]{3,2,1,0:T(1,128)S(1)}, u32[]{:S(2)}, u32[]{:S(2)}) collective-permute-start(f32[3,2,1,130]{3,2,1,0:T(1,128)S(1)} %get-tuple-element.96), channel_id=1, source_target_pairs={{0,1},{1,2},{2,3},{3,4},{4,5},{5,6},{6,7},{7,8},{8,9},{9,10},{10,1... | collective-permute-start | bytes 9368 | tf_op jit(solution)/shard_map/ppermute | solution.py:20
  37.5 1.6 copy-start.1
  39.1 42.1 %all-to-all-start = ((bf16[16,3,2,64,128]{4,3,2,1,0:T(8,128)(2,1)}), bf16[16,3,2,64,128]{4,3,2,1,0:T(8,128)(2,1)S(1)}, u32[]{:S(2)}, u32[]{:S(2)}) async-start(bf16[16,3,2,64,128]{4,3,2,1,0:T(8,128)(2,1)} %stack.18), calls=%async_computation | async-start | bytes 3145728 | tf_op jit(solution)/shard_map/all_to_all | solution.py:67
  82.9 14.5 %copy-start.3 = (s32[2,2048]{1,0:T(2,128)S(1)}, s32[2,2048]{1,0:T(2,128)}, u32[]{:S(2)}) copy-start(s32[2,2048]{1,0:T(2,128)} %param.11) | copy-start | bytes 49156
  85.9 20.3 %all-to-all-start.1 = ((bf16[32,2,768]{2,1,0:T(2,128)(2,1)}), bf16[32,2,768]{2,1,0:T(2,128)(2,1)S(1)}, u32[]{:S(2)}, u32[]{:S(2)}) async-start(bf16[32,2,768]{2,1,0:T(2,128)(2,1)} %reshape.96), calls=%async_computation.1 | async-start | bytes 196608 | tf_op jit(solution)/shard_map/all_to_all | solution.py:72
  183.1 122.9 %copy-start.4 = (f32[4,2,512]{2,1,0:T(2,128)}, f32[4,2,512]{2,1,0:T(2,128)S(1)}, u32[]{:S(2)}) copy-start(f32[4,2,512]{2,1,0:T(2,128)S(1)} %get-tuple-element.69) | copy-start | bytes 49156
